TPU v7x, 256 devices: a whole 4x4x8 slice. The times are simulated.
256 devices in a mesh: dom: 64 (over x, z, core), slab: 4 (over y).
Axes of the slice: x: 4, y: 4, z: 8, core: 2. Of those that a mesh axis runs over, the one named last changes fastest.
Arguments:
- logperm: float32 [256, 16, 64, 128], P('dom', 'slab'), may hold values from -4.2 to 4.2
- source: float32 [16, 64, 128], P('slab'), may hold values from -6 to 6
- observed: float32 [16, 64, 128], P('slab'), may hold values from -1.2 to 1.2
- brownian: float32 [256, 256], replicated, may hold values from -6 to 6
Outputs:
- particles_next: float32 [256, 16, 64, 128], P('dom', 'slab')
All inputs are finite; a program needn't handle non-finite values.
Results may differ from a plain program's by a relative error of at most 0.0003.
Values sent between devices are 32-bit elements; how exact they have to be, the bound alone decides.
No kernel may reach another device: no remote copies, remote signals or barrier semaphores. Data moves between devices by JAX's collectives and lax.ppermute only.
A program may use at most 64 MiB of HBM per device.

v0:
```python
import math
import jax
import jax.numpy as jnp
from jax import lax
from jax.sharding import PartitionSpec as P

SWEEPS = 8
misfit_weight = 1000.0


def with_halo(block, sides, width):
    for axis, dim in sides:
        count = lax.axis_size(axis)
        forward = [(i, i + 1) for i in range(count - 1)]
        backward = [(target, source) for source, target in forward]
        low = lax.ppermute(
            lax.slice_in_dim(block, block.shape[dim] - width, None, axis=dim), axis, forward
        )
        high = lax.ppermute(lax.slice_in_dim(block, 0, width, axis=dim), axis, backward)
        block = jnp.concatenate([low, block, high], axis=dim)
    return block


def neighbor_sum(core, below, above, fill):
    pad_y = jnp.pad(core, ((0, 0), (0, 0), (1, 1), (0, 0)), constant_values=fill)
    pad_z = jnp.pad(core, ((0, 0), (0, 0), (0, 0), (1, 1)), constant_values=fill)
    return below + above + pad_y[:, :, :-2] + pad_y[:, :, 2:] + pad_z[..., :-2] + pad_z[..., 2:]


def grad_field(e_core, e_below, e_above, p_core, p_below, p_above, q_core, q_below, q_above):
    summed = e_below * (p_core - p_below) * (q_core - q_below) + e_above * (p_core - p_above) * (
        q_core - q_above
    )
    for dimension in (2, 3):
        padding = [(0, 0), (0, 0), (0, 0), (0, 0)]
        padding[dimension] = (1, 1)
        e_pad = jnp.pad(e_core, padding, constant_values=1.0)
        p_pad = jnp.pad(p_core, padding)
        q_pad = jnp.pad(q_core, padding)
        extent = e_core.shape[dimension]
        for offset in (0, 2):
            e_near = lax.slice_in_dim(e_pad, offset, offset + extent, axis=dimension)
            p_near = lax.slice_in_dim(p_pad, offset, offset + extent, axis=dimension)
            q_near = lax.slice_in_dim(q_pad, offset, offset + extent, axis=dimension)
            summed = summed + e_near * (p_core - p_near) * (q_core - q_near)
    return -0.5 * e_core * summed


def on_device(logperm, source, observed, brownian):
    particles, width, rows_y, depth_z = logperm.shape
    slabs = lax.axis_size("slab")
    cells = width * slabs * rows_y * depth_z
    extended = with_halo(logperm, (("slab", 1),), 1)
    e_ext = jnp.exp(0.5 * extended)
    e_core = e_ext[:, 1:-1]
    inverse = 1.0 / neighbor_sum(e_core, e_ext[:, :-2], e_ext[:, 2:], 1.0)

    def relax_rim(rhs):
        value = inverse * rhs
        for sweep_index in range(SWEEPS - 1):
            bordered = with_halo(value, (("slab", 1),), 1)
            value = inverse * (
                rhs + e_core * neighbor_sum(value, bordered[:, :-2], bordered[:, 2:], 0.0)
            )
        return value / e_core

    pressure = relax_rim(source[None])
    misfit = misfit_weight * (pressure - observed[None])
    adjoint = relax_rim(misfit)
    states = with_halo(jnp.stack([pressure, adjoint]), (("slab", 2),), 1)
    gradient = grad_field(
        e_core,
        e_ext[:, :-2],
        e_ext[:, 2:],
        pressure,
        states[0][:, :-2],
        states[0][:, 2:],
        adjoint,
        states[1][:, :-2],
        states[1][:, 2:],
    )
    g_flat = gradient.reshape(particles, -1)
    u_cells, g_cells = (
        lax.all_to_all(
            logperm.reshape(particles, -1), "dom", split_axis=1, concat_axis=0, tiled=True
        ),
        lax.all_to_all(g_flat, "dom", split_axis=1, concat_axis=0, tiled=True),
    )
    ensemble = u_cells.shape[0]
    centre = jnp.mean(u_cells, axis=0, keepdims=True)
    spread = u_cells - centre
    partial_gram = lax.dot_general(
        spread,
        g_cells,
        (((1,), (1,)), ((), ())),
        precision=lax.Precision.HIGHEST,
        preferred_element_type=jnp.float32,
    )
    gram = lax.psum(partial_gram, ("dom", "slab"))
    step_size = ensemble / (4.0 * (cells + 1))
    mixing = -(step_size / ensemble) * gram + math.sqrt(2.0 * step_size / ensemble) * brownian
    moved = (
        centre
        + 1.25 * spread
        + lax.dot_general(
            mixing,
            spread,
            (((0,), (0,)), ((), ())),
            precision=lax.Precision.HIGHEST,
            preferred_element_type=jnp.float32,
        )
    )
    returned = lax.all_to_all(moved, "dom", split_axis=0, concat_axis=1, tiled=True)
    return returned.reshape(logperm.shape)


def solution(mesh):
    return jax.shard_map(
        on_device,
        mesh=mesh,
        in_specs=(P("dom", "slab", None, None), P("slab", None, None), P("slab", None, None), P()),
        out_specs=P("dom", "slab", None, None),
        check_vma=False,
    )
```

profile of v0, /device:TPU:1, one launch (start us, length us, event | category | flops | bytes accessed | tf_op | source)
XLA Modules:
  0.0 498.0 jit_solution(12891519340523834035)
XLA Ops:
  6.5 1.0 fusion.166
  7.6 4.0 collective-permute-start
  11.6 1.3 collective-permute-start.1
  13.7 3.6 collective-permute-done.1
  17.3 1.2 fusion
  18.9 3.2 collective-permute-start.2
  22.2 1.3 collective-permute-start.3
  24.1 3.8 collective-permute-done.3
  28.3 2.9 collective-permute-start.4
  31.2 1.3 collective-permute-start.5
  33.1 3.8 collective-permute-done.5
  37.3 2.2 collective-permute-start.6
  39.6 1.3 collective-permute-start.7
  41.5 3.8 collective-permute-done.7
  45.7 1.9 collective-permute-start.8
  47.6 1.3 collective-permute-start.9
  49.5 3.8 collective-permute-done.9
  53.7 1.9 collective-permute-start.10
  55.7 1.3 collective-permute-start.11
  57.6 3.8 collective-permute-done.11
  61.8 2.1 collective-permute-start.12
  63.9 1.3 collective-permute-start.13
  65.2 0.9 collective-permute-done.12
  66.1 4.1 collective-permute-done.13
  70.6 1.6 collective-permute-start.14
  72.3 1.3 collective-permute-start.15
  73.6 1.8 collective-permute-done.14
  75.3 3.9 collective-permute-done.15
  79.7 2.1 collective-permute-start.16
  81.9 1.3 collective-permute-start.17
  83.2 1.0 collective-permute-done.16
  84.2 3.8 collective-permute-done.17
  88.4 2.2 collective-permute-start.18
  90.7 1.3 collective-permute-start.19
  92.6 3.8 collective-permute-done.19
  96.9 2.2 collective-permute-start.20
  99.1 1.3 collective-permute-start.21
  101.0 3.8 collective-permute-done.21
  105.3 2.2 collective-permute-start.22
  107.5 1.3 collective-permute-start.23
  109.4 3.8 collective-permute-done.23
  113.7 1.9 collective-permute-start.24
  115.6 1.3 collective-permute-start.25
  117.5 3.8 collective-permute-done.25
  121.8 1.9 collective-permute-start.26
  123.8 1.3 collective-permute-start.27
  125.7 3.8 collective-permute-done.27
  130.0 1.9 collective-permute-start.28
  131.9 1.4 collective-permute-start.29
  133.8 3.9 collective-permute-done.29
  139.1 2.6 collective-permute-start.30
  141.7 1.3 collective-permute-start.31
  143.1 1.1 copy.7
  144.2 28.9 %all-to-all-start = ((f32[4,64,512]{2,0,1:T(4,128)}), f32[4,64,512]{2,0,1:T(4,128)S(1)}, u32[]{:S(2)}, u32[]{:S(2)}) async-start(f32[4,64,512]{2,0,1:T(4,128)} %copy.7), calls=%async_computation | async-start | bytes 1048576 | tf_op jit(solution)/shard_map/all_to_all | solution.py:84
  173.1 1.1 pad_maximum_fusion
  174.5 1.1 fusion.108
  175.6 1.1 copy.8
  176.8 13.7 %all-to-all-done = f32[4,64,512]{2,0,1:T(4,128)S(1)} async-done(((f32[4,64,512]{2,0,1:T(4,128)}), f32[4,64,512]{2,0,1:T(4,128)S(1)}, u32[]{:S(2)}, u32[]{:S(2)}) %all-to-all-start) | async-done | bytes 524320 | tf_op jit(solution)/shard_map/all_to_all | solution.py:84
  190.4 6.3 %all-to-all-start.1 = ((f32[4,64,512]{2,0,1:T(4,128)}), f32[4,64,512]{2,0,1:T(4,128)S(1)}, u32[]{:S(2)}, u32[]{:S(2)}) async-start(f32[4,64,512]{2,0,1:T(4,128)} %copy.8), calls=%async_computation.1 | async-start | bytes 1048576 | tf_op jit(solution)/shard_map/all_to_all | solution.py:87
  197.2 16.9 %all-to-all-done.1 = f32[4,64,512]{2,0,1:T(4,128)S(1)} async-done(((f32[4,64,512]{2,0,1:T(4,128)}), f32[4,64,512]{2,0,1:T(4,128)S(1)}, u32[]{:S(2)}, u32[]{:S(2)}) %all-to-all-start.1) | async-done | bytes 524320 | tf_op jit(solution)/shard_map/all_to_all | solution.py:87
  214.2 1.3 fusion.167
  215.8 245.4 %all-reduce.36.cloned.1.call-done = f32[256,256]{1,0:T(8,128)} async-done(((f32[256,256]{1,0:T(8,128)}), f32[256,256]{1,0:T(8,128)}) %all-reduce.36.cloned.1.call-update) | async-done | bytes 262160 | tf_op jit(solution)/shard_map/psum | solution.py:99
  461.1 1.6 convolution_add_fusion
  462.9 27.3 %all_to_all.54 = f32[64,4,512]{2,1,0:T(4,128)S(1)} all-to-all(f32[64,4,512]{2,1,0:T(4,128)S(1)} %all_to_all.48), channel_id=1, replica_groups=mesh['dom'=64,'slab'=4] {'dom'}, dimensions={0} | all-to-all | bytes 1048576 | tf_op jit(solution)/shard_map/all_to_all | solution.py:113
  (67 shorter events, 17.4 us)
Async XLA Ops:
  6.5 12.0 %copy-start.1 = (f32[4,64,128]{2,1,0:T(8,128)S(1)}, f32[4,64,128]{2,1,0:T(8,128)}, u32[]{:S(2)}) copy-start(f32[4,64,128]{2,1,0:T(8,128)} %param.5) | copy-start | bytes 393220
  7.6 6.2 %collective-permute-start = (f32[4,1,64,128]{3,2,1,0:T(8,128)S(1)}, f32[4,1,64,128]{3,2,1,0:T(8,128)S(1)}, u32[]{:S(2)}, u32[]{:S(2)}) collective-permute-start(f32[4,1,64,128]{3,2,1,0:T(8,128)S(1)} %get-tuple-element.41), channel_id=1, source_target_pairs={{0,1},{1,2},{2,3},{4,5},{5,6},{6,7},{8,9},{9,10},{10,11},{12,13},{... | collective-permute-start | bytes 393224 | tf_op jit(solution)/shard_map/ppermute | solution.py:16
  11.6 5.7 %collective-permute-start.1 = (f32[4,1,64,128]{3,2,1,0:T(8,128)S(1)}, f32[4,1,64,128]{3,2,1,0:T(8,128)S(1)}, u32[]{:S(2)}, u32[]{:S(2)}) collective-permute-start(f32[4,1,64,128]{3,2,1,0:T(8,128)S(1)} %get-tuple-element.42), channel_id=1, source_target_pairs={{1,0},{2,1},{3,2},{5,4},{6,5},{7,6},{9,8},{10,9},{11,10},{13,12},{... | collective-permute-start | bytes 393224 | tf_op jit(solution)/shard_map/ppermute | solution.py:19
  18.9 5.1 %collective-permute-start.2 = (f32[4,1,64,128]{3,2,1,0:T(8,128)S(1)}, f32[4,1,64,128]{3,2,1,0:T(8,128)S(1)}, u32[]{:S(2)}, u32[]{:S(2)}) collective-permute-start(f32[4,1,64,128]{3,2,1,0:T(8,128)S(1)} %get-tuple-element.39), channel_id=1, source_target_pairs={{0,1},{1,2},{2,3},{4,5},{5,6},{6,7},{8,9},{9,10},{10,11},{12,13},{... | collective-permute-start | bytes 393224 | tf_op jit(solution)/shard_map/ppermute | solution.py:16
  22.2 5.7 %collective-permute-start.3 = (f32[4,1,64,128]{3,2,1,0:T(8,128)S(1)}, f32[4,1,64,128]{3,2,1,0:T(8,128)S(1)}, u32[]{:S(2)}, u32[]{:S(2)}) collective-permute-start(f32[4,1,64,128]{3,2,1,0:T(8,128)S(1)} %get-tuple-element.40), channel_id=1, source_target_pairs={{1,0},{2,1},{3,2},{5,4},{6,5},{7,6},{9,8},{10,9},{11,10},{13,12},{... | collective-permute-start | bytes 393224 | tf_op jit(solution)/shard_map/ppermute | solution.py:19
  28.3 4.8 collective-permute-start.4
  31.2 5.7 %collective-permute-start.5 = (f32[4,1,64,128]{3,2,1,0:T(8,128)S(1)}, f32[4,1,64,128]{3,2,1,0:T(8,128)S(1)}, u32[]{:S(2)}, u32[]{:S(2)}) collective-permute-start(f32[4,1,64,128]{3,2,1,0:T(8,128)S(1)} %get-tuple-element.38), channel_id=1, source_target_pairs={{1,0},{2,1},{3,2},{5,4},{6,5},{7,6},{9,8},{10,9},{11,10},{13,12},{... | collective-permute-start | bytes 393224 | tf_op jit(solution)/shard_map/ppermute | solution.py:19
  37.3 4.1 collective-permute-start.6
  39.6 5.7 %collective-permute-start.7 = (f32[4,1,64,128]{3,2,1,0:T(8,128)S(1)}, f32[4,1,64,128]{3,2,1,0:T(8,128)S(1)}, u32[]{:S(2)}, u32[]{:S(2)}) collective-permute-start(f32[4,1,64,128]{3,2,1,0:T(8,128)S(1)} %get-tuple-element.36), channel_id=1, source_target_pairs={{1,0},{2,1},{3,2},{5,4},{6,5},{7,6},{9,8},{10,9},{11,10},{13,12},{... | collective-permute-start | bytes 393224 | tf_op jit(solution)/shard_map/ppermute | solution.py:19
  45.7 3.9 collective-permute-start.8
  47.6 5.7 %collective-permute-start.9 = (f32[4,1,64,128]{3,2,1,0:T(8,128)S(1)}, f32[4,1,64,128]{3,2,1,0:T(8,128)S(1)}, u32[]{:S(2)}, u32[]{:S(2)}) collective-permute-start(f32[4,1,64,128]{3,2,1,0:T(8,128)S(1)} %get-tuple-element.34), channel_id=1, source_target_pairs={{1,0},{2,1},{3,2},{5,4},{6,5},{7,6},{9,8},{10,9},{11,10},{13,12},{... | collective-permute-start | bytes 393224 | tf_op jit(solution)/shard_map/ppermute | solution.py:19
  53.7 3.9 collective-permute-start.10
  55.7 5.7 %collective-permute-start.11 = (f32[4,1,64,128]{3,2,1,0:T(8,128)S(1)}, f32[4,1,64,128]{3,2,1,0:T(8,128)S(1)}, u32[]{:S(2)}, u32[]{:S(2)}) collective-permute-start(f32[4,1,64,128]{3,2,1,0:T(8,128)S(1)} %get-tuple-element.32), channel_id=1, source_target_pairs={{1,0},{2,1},{3,2},{5,4},{6,5},{7,6},{9,8},{10,9},{11,10},{13,12},{... | collective-permute-start | bytes 393224 | tf_op jit(solution)/shard_map/ppermute | solution.py:19
  61.8 17.4 %copy-start = (f32[4,64,128]{2,1,0:T(8,128)S(1)}, f32[4,64,128]{2,1,0:T(8,128)}, u32[]{:S(2)}) copy-start(f32[4,64,128]{2,1,0:T(8,128)} %param.6) | copy-start | bytes 393220
  61.8 4.3 collective-permute-start.12
  63.9 6.3 %collective-permute-start.13 = (f32[4,1,64,128]{3,2,1,0:T(8,128)S(1)}, f32[4,1,64,128]{3,2,1,0:T(8,128)S(1)}, u32[]{:S(2)}, u32[]{:S(2)}) collective-permute-start(f32[4,1,64,128]{3,2,1,0:T(8,128)S(1)} %get-tuple-element.30), channel_id=1, source_target_pairs={{1,0},{2,1},{3,2},{5,4},{6,5},{7,6},{9,8},{10,9},{11,10},{13,12},{... | collective-permute-start | bytes 393224 | tf_op jit(solution)/shard_map/ppermute | solution.py:19
  70.6 4.7 collective-permute-start.14
  72.3 7.0 %collective-permute-start.15 = (f32[4,1,64,128]{3,2,1,0:T(8,128)S(1)}, f32[4,1,64,128]{3,2,1,0:T(8,128)S(1)}, u32[]{:S(2)}, u32[]{:S(2)}) collective-permute-start(f32[4,1,64,128]{3,2,1,0:T(8,128)S(1)} %get-tuple-element.28), channel_id=1, source_target_pairs={{1,0},{2,1},{3,2},{5,4},{6,5},{7,6},{9,8},{10,9},{11,10},{13,12},{... | collective-permute-start | bytes 393224 | tf_op jit(solution)/shard_map/ppermute | solution.py:19
  79.7 4.4 collective-permute-start.16
  81.9 6.1 %collective-permute-start.17 = (f32[4,1,64,128]{3,2,1,0:T(8,128)S(1)}, f32[4,1,64,128]{3,2,1,0:T(8,128)S(1)}, u32[]{:S(2)}, u32[]{:S(2)}) collective-permute-start(f32[4,1,64,128]{3,2,1,0:T(8,128)S(1)} %get-tuple-element.26), channel_id=1, source_target_pairs={{1,0},{2,1},{3,2},{5,4},{6,5},{7,6},{9,8},{10,9},{11,10},{13,12},{... | collective-permute-start | bytes 393224 | tf_op jit(solution)/shard_map/ppermute | solution.py:19
  88.4 4.2 collective-permute-start.18
  90.7 5.7 %collective-permute-start.19 = (f32[4,1,64,128]{3,2,1,0:T(8,128)S(1)}, f32[4,1,64,128]{3,2,1,0:T(8,128)S(1)}, u32[]{:S(2)}, u32[]{:S(2)}) collective-permute-start(f32[4,1,64,128]{3,2,1,0:T(8,128)S(1)} %get-tuple-element.24), channel_id=1, source_target_pairs={{1,0},{2,1},{3,2},{5,4},{6,5},{7,6},{9,8},{10,9},{11,10},{13,12},{... | collective-permute-start | bytes 393224 | tf_op jit(solution)/shard_map/ppermute | solution.py:19
  96.9 4.1 collective-permute-start.20
  99.1 5.7 %collective-permute-start.21 = (f32[4,1,64,128]{3,2,1,0:T(8,128)S(1)}, f32[4,1,64,128]{3,2,1,0:T(8,128)S(1)}, u32[]{:S(2)}, u32[]{:S(2)}) collective-permute-start(f32[4,1,64,128]{3,2,1,0:T(8,128)S(1)} %get-tuple-element.22), channel_id=1, source_target_pairs={{1,0},{2,1},{3,2},{5,4},{6,5},{7,6},{9,8},{10,9},{11,10},{13,12},{... | collective-permute-start | bytes 393224 | tf_op jit(solution)/shard_map/ppermute | solution.py:19
  105.3 4.1 collective-permute-start.22
  107.5 5.7 %collective-permute-start.23 = (f32[4,1,64,128]{3,2,1,0:T(8,128)S(1)}, f32[4,1,64,128]{3,2,1,0:T(8,128)S(1)}, u32[]{:S(2)}, u32[]{:S(2)}) collective-permute-start(f32[4,1,64,128]{3,2,1,0:T(8,128)S(1)} %get-tuple-element.20), channel_id=1, source_target_pairs={{1,0},{2,1},{3,2},{5,4},{6,5},{7,6},{9,8},{10,9},{11,10},{13,12},{... | collective-permute-start | bytes 393224 | tf_op jit(solution)/shard_map/ppermute | solution.py:19
  113.7 3.9 collective-permute-start.24
  115.6 5.7 %collective-permute-start.25 = (f32[4,1,64,128]{3,2,1,0:T(8,128)S(1)}, f32[4,1,64,128]{3,2,1,0:T(8,128)S(1)}, u32[]{:S(2)}, u32[]{:S(2)}) collective-permute-start(f32[4,1,64,128]{3,2,1,0:T(8,128)S(1)} %get-tuple-element.18), channel_id=1, source_target_pairs={{1,0},{2,1},{3,2},{5,4},{6,5},{7,6},{9,8},{10,9},{11,10},{13,12},{... | collective-permute-start | bytes 393224 | tf_op jit(solution)/shard_map/ppermute | solution.py:19
  121.8 3.9 collective-permute-start.26
  123.8 5.7 %collective-permute-start.27 = (f32[4,1,64,128]{3,2,1,0:T(8,128)S(1)}, f32[4,1,64,128]{3,2,1,0:T(8,128)S(1)}, u32[]{:S(2)}, u32[]{:S(2)}) collective-permute-start(f32[4,1,64,128]{3,2,1,0:T(8,128)S(1)} %get-tuple-element.16), channel_id=1, source_target_pairs={{1,0},{2,1},{3,2},{5,4},{6,5},{7,6},{9,8},{10,9},{11,10},{13,12},{... | collective-permute-start | bytes 393224 | tf_op jit(solution)/shard_map/ppermute | solution.py:19
  130.0 3.9 collective-permute-start.28
  131.9 11.1 %copy-start.2 = (f32[4,4,64,128]{3,2,1,0:T(8,128)S(1)}, f32[4,4,64,128]{3,2,1,0:T(8,128)}, u32[]{:S(2)}) copy-start(f32[4,4,64,128]{3,2,1,0:T(8,128)} %param.4) | copy-start | bytes 1572868
  131.9 5.8 %collective-permute-start.29 = (f32[4,1,64,128]{3,2,1,0:T(8,128)S(1)}, f32[4,1,64,128]{3,2,1,0:T(8,128)S(1)}, u32[]{:S(2)}, u32[]{:S(2)}) collective-permute-start(f32[4,1,64,128]{3,2,1,0:T(8,128)S(1)} %get-tuple-element.14), channel_id=1, source_target_pairs={{1,0},{2,1},{3,2},{5,4},{6,5},{7,6},{9,8},{10,9},{11,10},{13,12},{... | collective-permute-start | bytes 393224 | tf_op jit(solution)/shard_map/ppermute | solution.py:19
  139.1 34.0 %collective-permute-start.30 = (f32[2,4,1,64,128]{4,3,2,1,0:T(8,128)}, f32[2,4,1,64,128]{4,3,2,1,0:T(8,128)}, u32[]{:S(2)}, u32[]{:S(2)}) collective-permute-start(f32[2,4,1,64,128]{4,3,2,1,0:T(8,128)} %get-tuple-element.11), channel_id=1, source_target_pairs={{0,1},{1,2},{2,3},{4,5},{5,6},{6,7},{8,9},{9,10},{10,11},{12,13},{... | collective-permute-start | bytes 786440 | tf_op jit(solution)/shard_map/ppermute | solution.py:16
  141.7 31.4 %collective-permute-start.31 = (f32[2,4,1,64,128]{4,3,2,1,0:T(8,128)}, f32[2,4,1,64,128]{4,3,2,1,0:T(8,128)}, u32[]{:S(2)}, u32[]{:S(2)}) collective-permute-start(f32[2,4,1,64,128]{4,3,2,1,0:T(8,128)} %get-tuple-element.12), channel_id=1, source_target_pairs={{1,0},{2,1},{3,2},{5,4},{6,5},{7,6},{9,8},{10,9},{11,10},{13,12},{... | collective-permute-start | bytes 786440 | tf_op jit(solution)/shard_map/ppermute | solution.py:19
  144.2 46.2 %all-to-all-start = ((f32[4,64,512]{2,0,1:T(4,128)}), f32[4,64,512]{2,0,1:T(4,128)S(1)}, u32[]{:S(2)}, u32[]{:S(2)}) async-start(f32[4,64,512]{2,0,1:T(4,128)} %copy.7), calls=%async_computation | async-start | bytes 1048576 | tf_op jit(solution)/shard_map/all_to_all | solution.py:84
  190.4 23.6 %all-to-all-start.1 = ((f32[4,64,512]{2,0,1:T(4,128)}), f32[4,64,512]{2,0,1:T(4,128)S(1)}, u32[]{:S(2)}, u32[]{:S(2)}) async-start(f32[4,64,512]{2,0,1:T(4,128)} %copy.8), calls=%async_computation.1 | async-start | bytes 1048576 | tf_op jit(solution)/shard_map/all_to_all | solution.py:87
  196.7 264.4 %all-reduce.36.cloned.1.call-start = ((), (), s32[]{:S(2)}) async-start(), calls=%async_computation.3 | async-start | bytes 524288 | tf_op jit(solution)/shard_map/psum | solution.py:99
  214.2 246.9 %copy-start.3 = (f32[256,256]{1,0:T(8,128)S(1)}, f32[256,256]{1,0:T(8,128)}, u32[]{:S(2)}) copy-start(f32[256,256]{1,0:T(8,128)} %param.7) | copy-start | bytes 786436
Sparse Core Ops, SparseCore 0:
  215.7 245.3 all-reduce.35
where the time goes:
time: 499 us; the launch traced here: 498 us
  waiting for transfers between devices  344 us (69%)
  starting transfers between devices  93 us (19%)
  blocking collectives  27.3 us (5%)
  between operations  14.1 us (3%)
  other arithmetic  10.8 us (2%)
  local copies, waits for them, and re-layouts  5.66 us (1%)
    psum x1, waiting for transfers between devices, on_device(): gram = lax.psum(partial_gram, ('dom', 'slab'))  245 us
    ppermute x16, waiting for transfers between devices, with_halo(): lax.ppermute(lax.slice_in_dim(block, 0, width, axis=dim), axis, backward)  57.2 us
    ppermute x16, starting transfers between devices, with_halo(): lax.ppermute(lax.slice_in_dim(block, block.shape[dim] - width, None, axis...  37 us
    all_to_all x1, starting transfers between devices, on_device(): lax.all_to_all(logperm.reshape(particles, -1), 'dom', split_axis=1, conca...  28.9 us
    all_to_all x1, blocking collectives, on_device(): lax.all_to_all(moved, 'dom', split_axis=0, concat_axis=1, tiled=True)  27.3 us
    ppermute x16, starting transfers between devices, with_halo(): lax.ppermute(lax.slice_in_dim(block, 0, width, axis=dim), axis, backward)  20.8 us
    all_to_all x1, waiting for transfers between devices, on_device(): lax.all_to_all(g_flat, 'dom', split_axis=1, concat_axis=0, tiled=True)  16.9 us
    all_to_all x1, waiting for transfers between devices, on_device(): lax.all_to_all(logperm.reshape(particles, -1), 'dom', split_axis=1, conca...  13.7 us
  transfers between devices with their start and end apart: 35, of which 33 were waited for; matrix products, arithmetic and copies ran while one was open for 1% of the time, Pallas kernels for 0%

commit v1 on v0

--- a/solution.py
+++ b/solution.py
@@ -96,7 +96,7 @@
         precision=lax.Precision.HIGHEST,
         preferred_element_type=jnp.float32,
     )
-    gram = lax.psum(partial_gram, ("dom", "slab"))
+    gram = lax.psum(lax.psum(partial_gram, axis_name="slab"), axis_name="dom")
     step_size = ensemble / (4.0 * (cells + 1))
     mixing = -(step_size / ensemble) * gram + math.sqrt(2.0 * step_size / ensemble) * brownian
     moved = (

time: 499 us -> 473 us (0.948)
  waiting for transfers between devices: 344 us -> 322 us
    psum x1 -> x2, waiting for transfers between devices: 245 us -> 223 us  [on_device(): gram = lax.psum(lax.psum(partial_gram, axis_name='slab'), axis_name='dom')]
  transfers between devices with their start and end apart: 35 -> 36, of which waited for: 33 -> 34; matrix products, arithmetic and copies ran while one was open for 1% -> 1% of each run, Pallas kernels for 0% -> 0%
where the time goes in v1:
time: 473 us; the launch traced here: 472 us
  waiting for transfers between devices  322 us (68%)
  starting transfers between devices  93 us (20%)
  blocking collectives  23.7 us (5%)
  between operations  14.1 us (3%)
  other arithmetic  10.8 us (2%)
  local copies, waits for them, and re-layouts  5.66 us (1%)
    psum x2, waiting for transfers between devices, on_device(): gram = lax.psum(lax.psum(partial_gram, axis_name='slab'), axis_name='dom')  223 us
    ppermute x16, waiting for transfers between devices, with_halo(): lax.ppermute(lax.slice_in_dim(block, 0, width, axis=dim), axis, backward)  57.2 us
    ppermute x16, starting transfers between devices, with_halo(): lax.ppermute(lax.slice_in_dim(block, block.shape[dim] - width, None, axis...  37 us
    all_to_all x1, starting transfers between devices, on_device(): lax.all_to_all(logperm.reshape(particles, -1), 'dom', split_axis=1, conca...  28.9 us
    all_to_all x1, blocking collectives, on_device(): lax.all_to_all(moved, 'dom', split_axis=0, concat_axis=1, tiled=True)  23.7 us
    ppermute x16, starting transfers between devices, with_halo(): lax.ppermute(lax.slice_in_dim(block, 0, width, axis=dim), axis, backward)  20.8 us
    all_to_all x1, waiting for transfers between devices, on_device(): lax.all_to_all(g_flat, 'dom', split_axis=1, concat_axis=0, tiled=True)  16.9 us
    all_to_all x1, waiting for transfers between devices, on_device(): lax.all_to_all(logperm.reshape(particles, -1), 'dom', split_axis=1, conca...  13.7 us
  transfers between devices with their start and end apart: 36, of which 34 were waited for; matrix products, arithmetic and copies ran while one was open for 1% of the time, Pallas kernels for 0%

profile of v1, /device:TPU:1, one launch (start us, length us, event | category | flops | bytes accessed | tf_op | source)
XLA Modules:
  0.0 472.1 jit_solution(8300481808853504410)
XLA Ops:
  6.5 1.0 fusion.166
  7.6 4.0 collective-permute-start
  11.6 1.3 collective-permute-start.1
  13.7 3.6 collective-permute-done.1
  17.3 1.2 fusion
  18.9 3.2 collective-permute-start.2
  22.2 1.3 collective-permute-start.3
  24.1 3.8 collective-permute-done.3
  28.3 2.9 collective-permute-start.4
  31.2 1.3 collective-permute-start.5
  33.1 3.8 collective-permute-done.5
  37.3 2.2 collective-permute-start.6
  39.6 1.3 collective-permute-start.7
  41.5 3.8 collective-permute-done.7
  45.7 1.9 collective-permute-start.8
  47.6 1.3 collective-permute-start.9
  49.5 3.8 collective-permute-done.9
  53.7 1.9 collective-permute-start.10
  55.7 1.3 collective-permute-start.11
  57.6 3.8 collective-permute-done.11
  61.8 2.1 collective-permute-start.12
  63.9 1.3 collective-permute-start.13
  66.1 4.1 collective-permute-done.13
  70.6 1.6 collective-permute-start.14
  72.3 1.3 collective-permute-start.15
  73.6 1.8 collective-permute-done.14
  75.3 3.9 collective-permute-done.15
  79.7 2.1 collective-permute-start.16
  81.9 1.3 collective-permute-start.17
  83.2 1.0 collective-permute-done.16
  84.2 3.8 collective-permute-done.17
  88.4 2.2 collective-permute-start.18
  90.7 1.3 collective-permute-start.19
  92.6 3.8 collective-permute-done.19
  96.9 2.2 collective-permute-start.20
  99.1 1.3 collective-permute-start.21
  101.0 3.8 collective-permute-done.21
  105.3 2.2 collective-permute-start.22
  107.5 1.3 collective-permute-start.23
  109.4 3.8 collective-permute-done.23
  113.7 1.9 collective-permute-start.24
  115.6 1.3 collective-permute-start.25
  117.5 3.8 collective-permute-done.25
  121.8 1.9 collective-permute-start.26
  123.8 1.3 collective-permute-start.27
  125.7 3.8 collective-permute-done.27
  130.0 1.9 collective-permute-start.28
  131.9 1.4 collective-permute-start.29
  133.8 3.9 collective-permute-done.29
  139.1 2.6 collective-permute-start.30
  141.7 1.3 collective-permute-start.31
  143.1 1.1 copy.7
  144.2 28.9 %all-to-all-start = ((f32[4,64,512]{2,0,1:T(4,128)}), f32[4,64,512]{2,0,1:T(4,128)S(1)}, u32[]{:S(2)}, u32[]{:S(2)}) async-start(f32[4,64,512]{2,0,1:T(4,128)} %copy.7), calls=%async_computation | async-start | bytes 1048576 | tf_op jit(solution)/shard_map/all_to_all | solution.py:84
  173.1 1.1 pad_maximum_fusion
  174.5 1.1 fusion.108
  175.6 1.1 copy.8
  176.8 13.7 %all-to-all-done = f32[4,64,512]{2,0,1:T(4,128)S(1)} async-done(((f32[4,64,512]{2,0,1:T(4,128)}), f32[4,64,512]{2,0,1:T(4,128)S(1)}, u32[]{:S(2)}, u32[]{:S(2)}) %all-to-all-start) | async-done | bytes 524320 | tf_op jit(solution)/shard_map/all_to_all | solution.py:84
  190.4 6.3 %all-to-all-start.1 = ((f32[4,64,512]{2,0,1:T(4,128)}), f32[4,64,512]{2,0,1:T(4,128)S(1)}, u32[]{:S(2)}, u32[]{:S(2)}) async-start(f32[4,64,512]{2,0,1:T(4,128)} %copy.8), calls=%async_computation.1 | async-start | bytes 1048576 | tf_op jit(solution)/shard_map/all_to_all | solution.py:87
  197.2 16.9 %all-to-all-done.1 = f32[4,64,512]{2,0,1:T(4,128)S(1)} async-done(((f32[4,64,512]{2,0,1:T(4,128)}), f32[4,64,512]{2,0,1:T(4,128)S(1)}, u32[]{:S(2)}, u32[]{:S(2)}) %all-to-all-start.1) | async-done | bytes 524320 | tf_op jit(solution)/shard_map/all_to_all | solution.py:87
  214.2 1.3 fusion.167
  215.6 41.3 %all-reduce.37.cloned.1.call-done = f32[256,256]{1,0:T(8,128)} async-done(((f32[256,256]{1,0:T(8,128)}), f32[256,256]{1,0:T(8,128)}) %all-reduce.37.cloned.1.call-update) | async-done | bytes 262160 | tf_op jit(solution)/shard_map/psum | solution.py:99
  257.2 181.6 %all-reduce.39.cloned.1.call-done = f32[256,256]{1,0:T(8,128)} async-done(((f32[256,256]{1,0:T(8,128)}), f32[256,256]{1,0:T(8,128)}) %all-reduce.39.cloned.1.call-update) | async-done | bytes 262160 | tf_op jit(solution)/shard_map/psum | solution.py:99
  438.8 1.6 convolution_add_fusion
  440.6 23.7 %all_to_all.54 = f32[64,4,512]{2,1,0:T(4,128)S(1)} all-to-all(f32[64,4,512]{2,1,0:T(4,128)S(1)} %all_to_all.48), channel_id=1, replica_groups=mesh['dom'=64,'slab'=4] {'dom'}, dimensions={0} | all-to-all | bytes 1048576 | tf_op jit(solution)/shard_map/all_to_all | solution.py:113
  (70 shorter events, 18.4 us)
Async XLA Ops:
  6.5 12.0 %copy-start.1 = (f32[4,64,128]{2,1,0:T(8,128)S(1)}, f32[4,64,128]{2,1,0:T(8,128)}, u32[]{:S(2)}) copy-start(f32[4,64,128]{2,1,0:T(8,128)} %param.5) | copy-start | bytes 393220
  7.6 6.2 %collective-permute-start = (f32[4,1,64,128]{3,2,1,0:T(8,128)S(1)}, f32[4,1,64,128]{3,2,1,0:T(8,128)S(1)}, u32[]{:S(2)}, u32[]{:S(2)}) collective-permute-start(f32[4,1,64,128]{3,2,1,0:T(8,128)S(1)} %get-tuple-element.41), channel_id=1, source_target_pairs={{0,1},{1,2},{2,3},{4,5},{5,6},{6,7},{8,9},{9,10},{10,11},{12,13},{... | collective-permute-start | bytes 393224 | tf_op jit(solution)/shard_map/ppermute | solution.py:16
  11.6 5.7 %collective-permute-start.1 = (f32[4,1,64,128]{3,2,1,0:T(8,128)S(1)}, f32[4,1,64,128]{3,2,1,0:T(8,128)S(1)}, u32[]{:S(2)}, u32[]{:S(2)}) collective-permute-start(f32[4,1,64,128]{3,2,1,0:T(8,128)S(1)} %get-tuple-element.42), channel_id=1, source_target_pairs={{1,0},{2,1},{3,2},{5,4},{6,5},{7,6},{9,8},{10,9},{11,10},{13,12},{... | collective-permute-start | bytes 393224 | tf_op jit(solution)/shard_map/ppermute | solution.py:19
  18.9 5.1 %collective-permute-start.2 = (f32[4,1,64,128]{3,2,1,0:T(8,128)S(1)}, f32[4,1,64,128]{3,2,1,0:T(8,128)S(1)}, u32[]{:S(2)}, u32[]{:S(2)}) collective-permute-start(f32[4,1,64,128]{3,2,1,0:T(8,128)S(1)} %get-tuple-element.39), channel_id=1, source_target_pairs={{0,1},{1,2},{2,3},{4,5},{5,6},{6,7},{8,9},{9,10},{10,11},{12,13},{... | collective-permute-start | bytes 393224 | tf_op jit(solution)/shard_map/ppermute | solution.py:16
  22.2 5.7 %collective-permute-start.3 = (f32[4,1,64,128]{3,2,1,0:T(8,128)S(1)}, f32[4,1,64,128]{3,2,1,0:T(8,128)S(1)}, u32[]{:S(2)}, u32[]{:S(2)}) collective-permute-start(f32[4,1,64,128]{3,2,1,0:T(8,128)S(1)} %get-tuple-element.40), channel_id=1, source_target_pairs={{1,0},{2,1},{3,2},{5,4},{6,5},{7,6},{9,8},{10,9},{11,10},{13,12},{... | collective-permute-start | bytes 393224 | tf_op jit(solution)/shard_map/ppermute | solution.py:19
  28.3 4.8 %collective-permute-start.4 = (f32[4,1,64,128]{3,2,1,0:T(8,128)S(1)}, f32[4,1,64,128]{3,2,1,0:T(8,128)S(1)}, u32[]{:S(2)}, u32[]{:S(2)}) collective-permute-start(f32[4,1,64,128]{3,2,1,0:T(8,128)S(1)} %get-tuple-element.37), channel_id=1, source_target_pairs={{0,1},{1,2},{2,3},{4,5},{5,6},{6,7},{8,9},{9,10},{10,11},{12,13},{... | collective-permute-start | bytes 393224 | tf_op jit(solution)/shard_map/ppermute | solution.py:16
  31.2 5.7 %collective-permute-start.5 = (f32[4,1,64,128]{3,2,1,0:T(8,128)S(1)}, f32[4,1,64,128]{3,2,1,0:T(8,128)S(1)}, u32[]{:S(2)}, u32[]{:S(2)}) collective-permute-start(f32[4,1,64,128]{3,2,1,0:T(8,128)S(1)} %get-tuple-element.38), channel_id=1, source_target_pairs={{1,0},{2,1},{3,2},{5,4},{6,5},{7,6},{9,8},{10,9},{11,10},{13,12},{... | collective-permute-start | bytes 393224 | tf_op jit(solution)/shard_map/ppermute | solution.py:19
  37.3 4.1 collective-permute-start.6
  39.6 5.7 %collective-permute-start.7 = (f32[4,1,64,128]{3,2,1,0:T(8,128)S(1)}, f32[4,1,64,128]{3,2,1,0:T(8,128)S(1)}, u32[]{:S(2)}, u32[]{:S(2)}) collective-permute-start(f32[4,1,64,128]{3,2,1,0:T(8,128)S(1)} %get-tuple-element.36), channel_id=1, source_target_pairs={{1,0},{2,1},{3,2},{5,4},{6,5},{7,6},{9,8},{10,9},{11,10},{13,12},{... | collective-permute-start | bytes 393224 | tf_op jit(solution)/shard_map/ppermute | solution.py:19
  45.7 3.9 collective-permute-start.8
  47.6 5.7 %collective-permute-start.9 = (f32[4,1,64,128]{3,2,1,0:T(8,128)S(1)}, f32[4,1,64,128]{3,2,1,0:T(8,128)S(1)}, u32[]{:S(2)}, u32[]{:S(2)}) collective-permute-start(f32[4,1,64,128]{3,2,1,0:T(8,128)S(1)} %get-tuple-element.34), channel_id=1, source_target_pairs={{1,0},{2,1},{3,2},{5,4},{6,5},{7,6},{9,8},{10,9},{11,10},{13,12},{... | collective-permute-start | bytes 393224 | tf_op jit(solution)/shard_map/ppermute | solution.py:19
  53.7 3.9 collective-permute-start.10
  55.7 5.7 %collective-permute-start.11 = (f32[4,1,64,128]{3,2,1,0:T(8,128)S(1)}, f32[4,1,64,128]{3,2,1,0:T(8,128)S(1)}, u32[]{:S(2)}, u32[]{:S(2)}) collective-permute-start(f32[4,1,64,128]{3,2,1,0:T(8,128)S(1)} %get-tuple-element.32), channel_id=1, source_target_pairs={{1,0},{2,1},{3,2},{5,4},{6,5},{7,6},{9,8},{10,9},{11,10},{13,12},{... | collective-permute-start | bytes 393224 | tf_op jit(solution)/shard_map/ppermute | solution.py:19
  61.8 17.4 %copy-start = (f32[4,64,128]{2,1,0:T(8,128)S(1)}, f32[4,64,128]{2,1,0:T(8,128)}, u32[]{:S(2)}) copy-start(f32[4,64,128]{2,1,0:T(8,128)} %param.6) | copy-start | bytes 393220
  61.8 4.3 collective-permute-start.12
  63.9 6.3 %collective-permute-start.13 = (f32[4,1,64,128]{3,2,1,0:T(8,128)S(1)}, f32[4,1,64,128]{3,2,1,0:T(8,128)S(1)}, u32[]{:S(2)}, u32[]{:S(2)}) collective-permute-start(f32[4,1,64,128]{3,2,1,0:T(8,128)S(1)} %get-tuple-element.30), channel_id=1, source_target_pairs={{1,0},{2,1},{3,2},{5,4},{6,5},{7,6},{9,8},{10,9},{11,10},{13,12},{... | collective-permute-start | bytes 393224 | tf_op jit(solution)/shard_map/ppermute | solution.py:19
  70.6 4.7 collective-permute-start.14
  72.3 7.0 %collective-permute-start.15 = (f32[4,1,64,128]{3,2,1,0:T(8,128)S(1)}, f32[4,1,64,128]{3,2,1,0:T(8,128)S(1)}, u32[]{:S(2)}, u32[]{:S(2)}) collective-permute-start(f32[4,1,64,128]{3,2,1,0:T(8,128)S(1)} %get-tuple-element.28), channel_id=1, source_target_pairs={{1,0},{2,1},{3,2},{5,4},{6,5},{7,6},{9,8},{10,9},{11,10},{13,12},{... | collective-permute-start | bytes 393224 | tf_op jit(solution)/shard_map/ppermute | solution.py:19
  79.7 4.4 collective-permute-start.16
  81.9 6.1 %collective-permute-start.17 = (f32[4,1,64,128]{3,2,1,0:T(8,128)S(1)}, f32[4,1,64,128]{3,2,1,0:T(8,128)S(1)}, u32[]{:S(2)}, u32[]{:S(2)}) collective-permute-start(f32[4,1,64,128]{3,2,1,0:T(8,128)S(1)} %get-tuple-element.26), channel_id=1, source_target_pairs={{1,0},{2,1},{3,2},{5,4},{6,5},{7,6},{9,8},{10,9},{11,10},{13,12},{... | collective-permute-start | bytes 393224 | tf_op jit(solution)/shard_map/ppermute | solution.py:19
  88.4 4.2 collective-permute-start.18
  90.7 5.7 %collective-permute-start.19 = (f32[4,1,64,128]{3,2,1,0:T(8,128)S(1)}, f32[4,1,64,128]{3,2,1,0:T(8,128)S(1)}, u32[]{:S(2)}, u32[]{:S(2)}) collective-permute-start(f32[4,1,64,128]{3,2,1,0:T(8,128)S(1)} %get-tuple-element.24), channel_id=1, source_target_pairs={{1,0},{2,1},{3,2},{5,4},{6,5},{7,6},{9,8},{10,9},{11,10},{13,12},{... | collective-permute-start | bytes 393224 | tf_op jit(solution)/shard_map/ppermute | solution.py:19
  96.9 4.1 collective-permute-start.20
  99.1 5.7 %collective-permute-start.21 = (f32[4,1,64,128]{3,2,1,0:T(8,128)S(1)}, f32[4,1,64,128]{3,2,1,0:T(8,128)S(1)}, u32[]{:S(2)}, u32[]{:S(2)}) collective-permute-start(f32[4,1,64,128]{3,2,1,0:T(8,128)S(1)} %get-tuple-element.22), channel_id=1, source_target_pairs={{1,0},{2,1},{3,2},{5,4},{6,5},{7,6},{9,8},{10,9},{11,10},{13,12},{... | collective-permute-start | bytes 393224 | tf_op jit(solution)/shard_map/ppermute | solution.py:19
  105.3 4.1 collective-permute-start.22
  107.5 5.7 %collective-permute-start.23 = (f32[4,1,64,128]{3,2,1,0:T(8,128)S(1)}, f32[4,1,64,128]{3,2,1,0:T(8,128)S(1)}, u32[]{:S(2)}, u32[]{:S(2)}) collective-permute-start(f32[4,1,64,128]{3,2,1,0:T(8,128)S(1)} %get-tuple-element.20), channel_id=1, source_target_pairs={{1,0},{2,1},{3,2},{5,4},{6,5},{7,6},{9,8},{10,9},{11,10},{13,12},{... | collective-permute-start | bytes 393224 | tf_op jit(solution)/shard_map/ppermute | solution.py:19
  113.7 3.9 collective-permute-start.24
  115.6 5.7 %collective-permute-start.25 = (f32[4,1,64,128]{3,2,1,0:T(8,128)S(1)}, f32[4,1,64,128]{3,2,1,0:T(8,128)S(1)}, u32[]{:S(2)}, u32[]{:S(2)}) collective-permute-start(f32[4,1,64,128]{3,2,1,0:T(8,128)S(1)} %get-tuple-element.18), channel_id=1, source_target_pairs={{1,0},{2,1},{3,2},{5,4},{6,5},{7,6},{9,8},{10,9},{11,10},{13,12},{... | collective-permute-start | bytes 393224 | tf_op jit(solution)/shard_map/ppermute | solution.py:19
  121.8 3.9 collective-permute-start.26
  123.8 5.7 %collective-permute-start.27 = (f32[4,1,64,128]{3,2,1,0:T(8,128)S(1)}, f32[4,1,64,128]{3,2,1,0:T(8,128)S(1)}, u32[]{:S(2)}, u32[]{:S(2)}) collective-permute-start(f32[4,1,64,128]{3,2,1,0:T(8,128)S(1)} %get-tuple-element.16), channel_id=1, source_target_pairs={{1,0},{2,1},{3,2},{5,4},{6,5},{7,6},{9,8},{10,9},{11,10},{13,12},{... | collective-permute-start | bytes 393224 | tf_op jit(solution)/shard_map/ppermute | solution.py:19
  130.0 3.9 collective-permute-start.28
  131.9 11.1 %copy-start.2 = (f32[4,4,64,128]{3,2,1,0:T(8,128)S(1)}, f32[4,4,64,128]{3,2,1,0:T(8,128)}, u32[]{:S(2)}) copy-start(f32[4,4,64,128]{3,2,1,0:T(8,128)} %param.4) | copy-start | bytes 1572868
  131.9 5.8 %collective-permute-start.29 = (f32[4,1,64,128]{3,2,1,0:T(8,128)S(1)}, f32[4,1,64,128]{3,2,1,0:T(8,128)S(1)}, u32[]{:S(2)}, u32[]{:S(2)}) collective-permute-start(f32[4,1,64,128]{3,2,1,0:T(8,128)S(1)} %get-tuple-element.14), channel_id=1, source_target_pairs={{1,0},{2,1},{3,2},{5,4},{6,5},{7,6},{9,8},{10,9},{11,10},{13,12},{... | collective-permute-start | bytes 393224 | tf_op jit(solution)/shard_map/ppermute | solution.py:19
  139.1 34.0 %collective-permute-start.30 = (f32[2,4,1,64,128]{4,3,2,1,0:T(8,128)}, f32[2,4,1,64,128]{4,3,2,1,0:T(8,128)}, u32[]{:S(2)}, u32[]{:S(2)}) collective-permute-start(f32[2,4,1,64,128]{4,3,2,1,0:T(8,128)} %get-tuple-element.11), channel_id=1, source_target_pairs={{0,1},{1,2},{2,3},{4,5},{5,6},{6,7},{8,9},{9,10},{10,11},{12,13},{... | collective-permute-start | bytes 786440 | tf_op jit(solution)/shard_map/ppermute | solution.py:16
  141.7 31.4 %collective-permute-start.31 = (f32[2,4,1,64,128]{4,3,2,1,0:T(8,128)}, f32[2,4,1,64,128]{4,3,2,1,0:T(8,128)}, u32[]{:S(2)}, u32[]{:S(2)}) collective-permute-start(f32[2,4,1,64,128]{4,3,2,1,0:T(8,128)} %get-tuple-element.12), channel_id=1, source_target_pairs={{1,0},{2,1},{3,2},{5,4},{6,5},{7,6},{9,8},{10,9},{11,10},{13,12},{... | collective-permute-start | bytes 786440 | tf_op jit(solution)/shard_map/ppermute | solution.py:19
  144.2 46.2 %all-to-all-start = ((f32[4,64,512]{2,0,1:T(4,128)}), f32[4,64,512]{2,0,1:T(4,128)S(1)}, u32[]{:S(2)}, u32[]{:S(2)}) async-start(f32[4,64,512]{2,0,1:T(4,128)} %copy.7), calls=%async_computation | async-start | bytes 1048576 | tf_op jit(solution)/shard_map/all_to_all | solution.py:84
  190.4 23.6 %all-to-all-start.1 = ((f32[4,64,512]{2,0,1:T(4,128)}), f32[4,64,512]{2,0,1:T(4,128)S(1)}, u32[]{:S(2)}, u32[]{:S(2)}) async-start(f32[4,64,512]{2,0,1:T(4,128)} %copy.8), calls=%async_computation.1 | async-start | bytes 1048576 | tf_op jit(solution)/shard_map/all_to_all | solution.py:87
  196.7 60.2 %all-reduce.37.cloned.1.call-start = ((), (), s32[]{:S(2)}) async-start(), calls=%async_computation.3 | async-start | bytes 524288 | tf_op jit(solution)/shard_map/psum | solution.py:99
  214.2 224.5 %copy-start.3 = (f32[256,256]{1,0:T(8,128)S(1)}, f32[256,256]{1,0:T(8,128)}, u32[]{:S(2)}) copy-start(f32[256,256]{1,0:T(8,128)} %param.7) | copy-start | bytes 786436
  215.6 223.2 %all-reduce.39.cloned.1.call-start = ((), (), s32[]{:S(2)}) async-start(), calls=%async_computation.4 | async-start | bytes 524288 | tf_op jit(solution)/shard_map/psum | solution.py:99
Sparse Core Ops, SparseCore 0:
  215.7 41.1 all-reduce.36
  260.8 177.8 all-reduce.38
